TPU v7x, 32 devices: a whole 2x2x4 slice. The times are simulated.
32 devices in a mesh: dp: 8 (over z, y), tensor: 4 (over x, core).
Axes of the slice: x: 2, y: 2, z: 4, core: 2. Of those that a mesh axis runs over, the one named last changes fastest.
Arguments:
- tokens: bfloat16 [8192, 768], P('dp'), may hold values from -6 to 6
- segment_ids: int32 [16, 512], P('dp'), may hold values from 0 to 3, never falling along the last dimension, each value on 1 to 256 neighbouring positions
- qkv_weight: bfloat16 [768, 3, 12, 64], P(None, None, 'tensor'), may hold values from -0.21875 to 0.21875
- qkv_bias: bfloat16 [2, 12, 64], P(None, 'tensor'), may hold values from -3 to 3
- output_weight: bfloat16 [12, 64, 768], P('tensor'), may hold values from -1.25 to 1.25
- output_bias: bfloat16 [768], replicated, may hold values from -2 to 2
- first_gain: bfloat16 [768], replicated, may hold values from 0.5 to 1.5
- first_shift: bfloat16 [768], replicated, may hold values from -2 to 2
- up_weight: bfloat16 [768, 3072], P(None, 'tensor'), may hold values from -0.21875 to 0.21875
- up_bias: bfloat16 [48, 64], P('tensor'), may hold values from -3 to 3
- down_weight: bfloat16 [3072, 768], P('tensor'), may hold values from -0.109375 to 0.109375
- down_bias: bfloat16 [768], replicated, may hold values from -2 to 2
- second_gain: bfloat16 [768], replicated, may hold values from 0.5 to 1.5
- second_shift: bfloat16 [768], replicated, may hold values from -2 to 2
- cotangent: bfloat16 [8192, 768], P('dp'), may hold values from -6 to 6
Outputs:
- layer_out: bfloat16 [8192, 768], P(('dp', 'tensor'))
- tokens_grad: bfloat16 [8192, 768], P(('dp', 'tensor'))
- qkv_weight_grad: float32 [768, 3, 12, 64], P('dp', None, 'tensor')
- qkv_bias_grad: float32 [2, 12, 64], P(None, 'tensor', 'dp')
- output_weight_grad: float32 [12, 64, 768], P('tensor', None, 'dp')
- output_bias_grad: float32 [768], P('dp')
- first_gain_grad: float32 [768], P('dp')
- first_shift_grad: float32 [768], P('dp')
- up_weight_grad: float32 [768, 3072], P('dp', 'tensor')
- up_bias_grad: float32 [48, 64], P('tensor', 'dp')
- down_weight_grad: float32 [3072, 768], P('tensor', 'dp')
- down_bias_grad: float32 [768], P('dp')
- second_gain_grad: float32 [768], P('dp')
- second_shift_grad: float32 [768], P('dp')
Inputs may be any that keep to these rules, and one draw needn't show every extreme that they name: `segment_ids`: along each row of 512 tokens the ids never fall; each id covers 1 to 256 tokens of its row.
All inputs are finite; a program needn't handle non-finite values.
Results may differ from a plain program's by a relative error of at most 0.02.
The roundings to bfloat16 on the way count: a program that leaves them out, or rounds other values in their place, can miss the bound.
Values may be sent and summed in bfloat16 or wider, within the bound.
A program may use at most 128 MiB of HBM per device.

v0:
```python
import jax
import jax.numpy as jnp
from jax import lax
from jax.sharding import PartitionSpec as P

HEAD = 64
SEQ = 512
EPS = 1e-12


def normalize(rows_in, gain_vec, shift_vec):
    center = rows_in - jnp.mean(rows_in, axis=-1, keepdims=True)
    spread = jnp.mean(center * center, axis=-1, keepdims=True)
    return center * lax.rsqrt(spread + EPS) * gain_vec + shift_vec


def norm_back(rows_in, gain_vec, shift_vec, grad_out):
    unused, pull_back = jax.vjp(normalize, rows_in, gain_vec, shift_vec)
    return pull_back(grad_out)


def gelu_exact(values_in):
    return jax.nn.gelu(values_in, approximate=False)


def head_scores(queries, keys_low, same_doc):
    scores = jnp.einsum(
        "rqhd,rkhd->rhqk", queries, keys_low, preferred_element_type=jnp.float32
    ) * HEAD ** (-0.5)
    return jnp.where(same_doc[:, None], scores, -1e30)


def attend(queries, keys_low, values_low, same_doc):
    scores = head_scores(queries, keys_low, same_doc)
    row_top = jnp.max(scores, axis=-1, keepdims=True)
    expo_vals = jnp.exp(scores - row_top)
    row_total = jnp.sum(expo_vals, axis=-1, keepdims=True)
    attn_probs = (expo_vals / row_total).astype(jnp.bfloat16)
    context = jnp.einsum(
        "rhqk,rkhd->rqhd", attn_probs, values_low, preferred_element_type=jnp.float32
    )
    return (context.astype(jnp.bfloat16), row_top + jnp.log(row_total))


def attend_back(queries, keys_low, values_low, same_doc, log_total, d_context):
    probs_full = jnp.exp(head_scores(queries, keys_low, same_doc) - log_total)
    d_probs = jnp.einsum(
        "rqhd,rkhd->rhqk", d_context, values_low, preferred_element_type=jnp.float32
    )
    inner_sum = jnp.sum(probs_full * d_probs, axis=-1, keepdims=True)
    d_scores = (probs_full * (d_probs - inner_sum)).astype(jnp.bfloat16)
    factor = HEAD ** (-0.5)
    d_query = (
        jnp.einsum("rhqk,rkhd->rqhd", d_scores, keys_low, preferred_element_type=jnp.float32)
        * factor
    )
    d_keys = (
        jnp.einsum("rhqk,rqhd->rkhd", d_scores, queries, preferred_element_type=jnp.float32)
        * factor
    )
    d_values = jnp.einsum(
        "rhqk,rqhd->rkhd",
        probs_full.astype(jnp.bfloat16),
        d_context,
        preferred_element_type=jnp.float32,
    )
    return (d_query, d_keys, d_values)


def body(
    tokens,
    segment_ids,
    qkv_weight,
    qkv_bias,
    output_weight,
    output_bias,
    first_gain,
    first_shift,
    up_weight,
    up_bias,
    down_weight,
    down_bias,
    second_gain,
    second_shift,
    cotangent,
):
    token_count = tokens.shape[0]
    row_count = token_count // SEQ
    head_count = qkv_weight.shape[2]
    head_width = head_count * HEAD
    share_rows = token_count // lax.axis_size("tensor")
    offset = lax.axis_index("tensor") * share_rows
    same_doc = segment_ids[:, :, None] == segment_ids[:, None, :]
    qkv_matrix = qkv_weight.reshape(qkv_weight.shape[0], 3 * head_width)
    out_matrix = output_weight.reshape(head_width, output_weight.shape[2])
    bias_rows = qkv_bias.astype(jnp.float32).reshape(2, head_width)
    gain_first = first_gain.astype(jnp.float32)
    shift_first = first_shift.astype(jnp.float32)
    gain_second = second_gain.astype(jnp.float32)
    shift_second = second_shift.astype(jnp.float32)

    def split_heads(matrix):
        return matrix.reshape(row_count, SEQ, head_count, HEAD)

    mixed_proj = jnp.dot(tokens, qkv_matrix, preferred_element_type=jnp.float32).reshape(
        token_count, 3, head_width
    )
    queries = (mixed_proj[:, 0] + bias_rows[0]).astype(jnp.bfloat16)
    keys_low = mixed_proj[:, 1].astype(jnp.bfloat16)
    values_low = (mixed_proj[:, 2] + bias_rows[1]).astype(jnp.bfloat16)
    context, log_total = attend(
        split_heads(queries), split_heads(keys_low), split_heads(values_low), same_doc
    )
    context = context.reshape(token_count, head_width)
    attn_terms = jnp.dot(context, out_matrix, preferred_element_type=jnp.float32)
    attn_total = lax.psum(attn_terms.astype(jnp.bfloat16), "tensor").astype(jnp.float32)
    residual = tokens.astype(jnp.float32)
    grad_rows = cotangent.astype(jnp.float32)
    first_in = residual + attn_total + output_bias.astype(jnp.float32)
    first_out = normalize(first_in, gain_first, shift_first)
    first_low = first_out.astype(jnp.bfloat16)
    hidden = jnp.dot(first_low, up_weight, preferred_element_type=jnp.float32) + up_bias.astype(
        jnp.float32
    ).reshape(-1)
    active, gelu_pull = jax.vjp(gelu_exact, hidden)
    active_low = active.astype(jnp.bfloat16)
    down_terms = jnp.dot(active_low, down_weight, preferred_element_type=jnp.float32)
    down_total = lax.psum(down_terms.astype(jnp.bfloat16), "tensor").astype(jnp.float32)
    second_in = first_out + down_total + down_bias.astype(jnp.float32)
    layer_full = normalize(second_in, gain_second, shift_second).astype(jnp.bfloat16)
    d_second, gain_second_grad, shift_second_grad = norm_back(
        second_in, gain_second, shift_second, grad_rows
    )
    down_bias_grad = jnp.sum(d_second, axis=0)
    d_second_low = d_second.astype(jnp.bfloat16)
    down_grad = jnp.einsum(
        "tf,td->fd", active_low, d_second_low, preferred_element_type=jnp.float32
    )
    d_active = jnp.einsum(
        "td,fd->tf", d_second_low, down_weight, preferred_element_type=jnp.float32
    )
    (d_hidden,) = gelu_pull(d_active)
    up_bias_grad = jnp.sum(d_hidden, axis=0).reshape(up_bias.shape)
    d_hidden_low = d_hidden.astype(jnp.bfloat16)
    up_grad = jnp.einsum("td,tf->df", first_low, d_hidden_low, preferred_element_type=jnp.float32)
    up_terms = jnp.einsum("tf,df->td", d_hidden_low, up_weight, preferred_element_type=jnp.float32)
    up_total = lax.psum(up_terms.astype(jnp.bfloat16), "tensor").astype(jnp.float32)
    d_first = d_second + up_total
    d_first_in, gain_first_grad, shift_first_grad = norm_back(
        first_in, gain_first, shift_first, d_first
    )
    out_bias_grad = jnp.sum(d_first_in, axis=0)
    d_attn_low = d_first_in.astype(jnp.bfloat16)
    out_grad = jnp.einsum("tc,td->cd", context, d_attn_low, preferred_element_type=jnp.float32)
    d_context = jnp.einsum(
        "td,cd->tc", d_attn_low, out_matrix, preferred_element_type=jnp.float32
    ).astype(jnp.bfloat16)
    d_query, d_keys, d_values = attend_back(
        split_heads(queries),
        split_heads(keys_low),
        split_heads(values_low),
        same_doc,
        log_total,
        split_heads(d_context),
    )
    d_query = d_query.reshape(token_count, head_width)
    d_keys = d_keys.reshape(token_count, head_width)
    d_values = d_values.reshape(token_count, head_width)
    qkv_bias_grad = jnp.stack([jnp.sum(d_query, axis=0), jnp.sum(d_values, axis=0)]).reshape(
        qkv_bias.shape
    )
    d_mixed = (
        jnp.stack([d_query, d_keys, d_values], axis=1)
        .astype(jnp.bfloat16)
        .reshape(token_count, 3 * head_width)
    )
    qkv_grad = jnp.einsum("td,tc->dc", tokens, d_mixed, preferred_element_type=jnp.float32).reshape(
        qkv_weight.shape
    )
    token_terms = jnp.einsum("tc,dc->td", d_mixed, qkv_matrix, preferred_element_type=jnp.float32)
    token_total = lax.psum(token_terms.astype(jnp.bfloat16), "tensor").astype(jnp.float32)
    tokens_grad = lax.dynamic_slice_in_dim(d_first_in + token_total, offset, share_rows, 0).astype(
        jnp.bfloat16
    )
    layer_out = lax.dynamic_slice_in_dim(layer_full, offset, share_rows, 0)
    small_grads = (
        out_bias_grad,
        gain_first_grad,
        shift_first_grad,
        down_bias_grad,
        gain_second_grad,
        shift_second_grad,
    )
    attn_parts = (
        lax.psum_scatter(qkv_grad, "dp", scatter_dimension=0, tiled=True),
        lax.psum_scatter(qkv_bias_grad, "dp", scatter_dimension=2, tiled=True),
        lax.psum_scatter(
            out_grad.reshape(output_weight.shape), "dp", scatter_dimension=2, tiled=True
        ),
        lax.psum_scatter(small_grads[0], "dp", scatter_dimension=0, tiled=True),
        lax.psum_scatter(small_grads[1], "dp", scatter_dimension=0, tiled=True),
        lax.psum_scatter(small_grads[2], "dp", scatter_dimension=0, tiled=True),
    )
    ffn_parts = (
        lax.psum_scatter(up_grad, "dp", scatter_dimension=0, tiled=True),
        lax.psum_scatter(up_bias_grad, "dp", scatter_dimension=1, tiled=True),
        lax.psum_scatter(down_grad, "dp", scatter_dimension=1, tiled=True),
        lax.psum_scatter(small_grads[3], "dp", scatter_dimension=0, tiled=True),
        lax.psum_scatter(small_grads[4], "dp", scatter_dimension=0, tiled=True),
        lax.psum_scatter(small_grads[5], "dp", scatter_dimension=0, tiled=True),
    )
    return (
        layer_out,
        tokens_grad,
        attn_parts[0],
        attn_parts[1],
        attn_parts[2],
        attn_parts[3],
        attn_parts[4],
        attn_parts[5],
        ffn_parts[0],
        ffn_parts[1],
        ffn_parts[2],
        ffn_parts[3],
        ffn_parts[4],
        ffn_parts[5],
    )


def solution(mesh):
    placed = (
        P("dp", None),
        P("dp", None),
        P(None, None, "tensor", None),
        P(None, "tensor", None),
        P("tensor", None, None),
        P(),
        P(),
        P(),
        P(None, "tensor"),
        P("tensor", None),
        P("tensor", None),
        P(),
        P(),
        P(),
        P("dp", None),
    )
    return jax.shard_map(
        body,
        mesh=mesh,
        in_specs=placed,
        out_specs=(
            P(("dp", "tensor"), None),
            P(("dp", "tensor"), None),
            P("dp", None, "tensor", None),
            P(None, "tensor", "dp"),
            P("tensor", None, "dp"),
            P("dp"),
            P("dp"),
            P("dp"),
            P("dp", "tensor"),
            P("tensor", "dp"),
            P("tensor", "dp"),
            P("dp"),
            P("dp"),
            P("dp"),
        ),
        check_vma=False,
    )
```

profile of v0, /device:TPU:0, one launch (start us, length us, event | category | flops | bytes accessed | tf_op | source)
XLA Modules:
  0.0 553.5 jit_solution(17935516750213851059)
XLA Ops:
  7.2 2.8 fusion.21
  10.2 1.0 fusion.64
  11.2 1.2 broadcast_compare_fusion
  13.4 2.1 squeeze.8
  15.5 2.5 fusion.66
  19.0 1.6 copy-done.2
  20.7 1.3 fusion.29
  23.3 1.9 convolution_convert_fusion.3
  25.8 1.3 convert_element_type.130
  27.7 43.2 %all-reduce.14.cloned.1.call-done = bf16[1024,768]{1,0:T(8,128)(2,1)} async-done(((bf16[1024,768]{1,0:T(8,128)(2,1)}), bf16[1024,768]{1,0:T(8,128)(2,1)}) %all-reduce.14.cloned.1.call-update) | async-done | bytes 1572880 | tf_op jit(solution)/shard_map/psum | solution.py:116
  70.9 2.1 fusion.17
  74.6 9.9 %multiply_convert_fusion.1 = (bf16[1024,768]{1,0:T(8,128)(2,1)S(1)}, f32[1024,768]{1,0:T(8,128)}, f32[1024,768]{1,0:T(8,128)}) fusion(f32[768]{0:T(1024)S(1)} %copy-done.57, bf16[768,768]{1,0:T(8,128)(2,1)S(1)} %copy-done, f32[768]{0:T(1024)S(1)} %copy-done.47, f32[768]{0:T(1024)S(1)} %convert_element_type.129, f32[1024]{0:T(1024)S(1)} %fusion.49, ...), kind=kOutput, calls=%fused_computation.27 | convolution fusion | flops 1266941952 | bytes 12210176 | tf_op jit(solution)/shard_map/dot_general | solution.py:122
  84.5 1.2 copy-done.65
  85.7 2.5 convolution_convert_fusion.2
  88.3 1.3 convert_element_type.136
  89.6 1.3 convert_element_type.135
  90.8 40.5 %all-reduce.16.cloned.1.call-done = bf16[1024,768]{1,0:T(8,128)(2,1)} async-done(((bf16[1024,768]{1,0:T(8,128)(2,1)}), bf16[1024,768]{1,0:T(8,128)(2,1)}) %all-reduce.16.cloned.1.call-update) | async-done | bytes 1572880 | tf_op jit(solution)/shard_map/psum | solution.py:128
  131.4 3.3 fusion.62
  134.7 1.8 fusion.4
  136.5 3.6 fusion.61
  140.8 3.2 fusion.69
  144.0 1.2 copy-done.68
  145.2 2.6 convolution_convert_fusion.1
  148.7 42.2 %all-reduce.18.cloned.1.call-done = bf16[1024,768]{1,0:T(8,128)(2,1)} async-done(((bf16[1024,768]{1,0:T(8,128)(2,1)}), bf16[1024,768]{1,0:T(8,128)(2,1)}) %all-reduce.18.cloned.1.call-update) | async-done | bytes 1572880 | tf_op jit(solution)/shard_map/psum | solution.py:147
  190.9 4.5 fusion.59
  195.4 2.6 multiply_reduce_fusion.1
  198.1 2.1 fusion.60
  200.2 1.8 copy-done.6
  202.9 5.4 fusion.67
  208.3 4.5 multiply_reduce_fusion
  212.9 1.8 multiply_convert_fusion
  214.7 1.1 fusion.26
  219.8 3.8 convolution_convert_fusion
  223.6 2.4 fusion.19
  226.0 1.5 copy.79
  227.5 2.8 reshape.190
  230.4 2.3 convolution_bitcast_fusion
  232.7 3.0 copy.83
  235.9 5.4 fusion.51
  241.4 5.2 fusion.37
  248.8 2.0 fusion.32
  250.8 37.6 %all-reduce.8 = (f32[2,3,64]{2,1,0:T(4,128)S(1)}, f32[768]{0:T(1024)S(1)}, f32[768]{0:T(1024)S(1)}, f32[768]{0:T(1024)S(1)}, f32[12,64]{1,0:T(8,128)S(1)}, /*ind...) all-reduce(f32[2,3,64]{2,1,0:T(4,128)S(1)} %pad_maximum_fusion, ...), channel_id=3, replica_groups=mesh['dp'=8,'tensor'=4] {'dp'}, use_global_device_ids=true, to_apply=%region_18.19.clone | all-reduce | flops 5760 | bytes 46080
  293.2 2.1 fusion.30
  295.3 37.1 %reduce-scatter.17.cloned.1.call-done = f32[96,192]{1,0:T(8,128)} async-done(((f32[768,192]{1,0:T(8,128)}), f32[96,192]{1,0:T(8,128)}) %reduce-scatter.17.cloned.1.call-update) | async-done | bytes 73744
  334.2 67.8 %reduce-scatter.15.cloned.1.call-done = f32[96,576]{1,0:T(8,128)} async-done(((f32[768,576]{1,0:T(8,128)}), f32[96,576]{1,0:T(8,128)}) %reduce-scatter.15.cloned.1.call-update) | async-done | bytes 221200
  401.9 1.8 copy.84
  403.8 70.4 %reduce-scatter.13.cloned.1.call-done = f32[768,96]{0,1:T(8,128)} async-done(((f32[768,768]{0,1:T(8,128)}), f32[768,96]{0,1:T(8,128)}) %reduce-scatter.13.cloned.1.call-update) | async-done | bytes 294928 | tf_op jit(solution)/shard_map/reduce_scatter | solution.py:207
  474.1 72.3 %reduce-scatter.11.cloned.1.call-done = f32[96,768]{1,0:T(8,128)} async-done(((f32[768,768]{1,0:T(8,128)}), f32[96,768]{1,0:T(8,128)}) %reduce-scatter.11.cloned.1.call-update) | async-done | bytes 294928 | tf_op jit(solution)/shard_map/reduce_scatter | solution.py:205
  (202 shorter events, 20.2 us)
Async XLA Ops:
  7.2 67.4 %copy-start = (bf16[768,768]{1,0:T(8,128)(2,1)S(1)}, bf16[768,768]{1,0:T(8,128)(2,1)}, u32[]{:S(2)}) copy-start(bf16[768,768]{1,0:T(8,128)(2,1)} %param.23) | copy-start | bytes 3538948
  7.2 63.7 %all-reduce.14.cloned.1.call-start = ((), (), s32[]{:S(2)}) async-start(), calls=%async_computation.4 | async-start | bytes 3145728 | tf_op jit(solution)/shard_map/psum | solution.py:116
  12.7 5.3 copy-start.9
  13.4 5.6 %copy-start.13 = (f32[2,512,3,64]{1,0,3,2:T(2,128)}, f32[2,512,3,64]{1,0,3,2:T(2,128)S(1)}, u32[]{:S(2)}) copy-start(f32[2,512,3,64]{1,0,3,2:T(2,128)S(1)} %squeeze.7) | copy-start | bytes 2359300
  22.1 5.0 copy-start.56
  22.1 48.8 %copy-start.3 = (bf16[1024,768]{1,0:T(8,128)(2,1)S(1)}, bf16[1024,768]{1,0:T(8,128)(2,1)}, u32[]{:S(2)}) copy-start(bf16[1024,768]{1,0:T(8,128)(2,1)} %param.15) | copy-start | bytes 4718596
  25.2 106.1 %all-reduce.16.cloned.1.call-start = ((), (), s32[]{:S(2)}) async-start(), calls=%async_computation.5 | async-start | bytes 3145728 | tf_op jit(solution)/shard_map/psum | solution.py:128
  25.8 105.6 %copy-start.20 = (f32[768]{0:T(1024)}, f32[768]{0:T(1024)S(1)}, u32[]{:S(2)}) copy-start(f32[768]{0:T(1024)S(1)} %convert_element_type.128) | copy-start | bytes 9220
  25.8 105.5 %copy-start.27 = (f32[768]{0:T(1024)}, f32[768]{0:T(1024)S(1)}, u32[]{:S(2)}) copy-start(f32[768]{0:T(1024)S(1)} %convert_element_type.129) | copy-start | bytes 9220
  73.0 58.3 %copy-start.23 = (f32[1024]{0:T(1024)}, f32[1024]{0:T(1024)S(1)}, u32[]{:S(2)}) copy-start(f32[1024]{0:T(1024)S(1)} %broadcast_multiply_fusion.1) | copy-start | bytes 12292
  74.6 56.8 %copy-start.30 = (f32[1024]{0:T(1024)}, f32[1024]{0:T(1024)S(1)}, u32[]{:S(2)}) copy-start(f32[1024]{0:T(1024)S(1)} %fusion.49) | copy-start | bytes 12292
  74.6 11.1 %copy-start.62 = (bf16[768,768]{1,0:T(8,128)(2,1)S(1)}, bf16[768,768]{1,0:T(8,128)(2,1)}, u32[]{:S(2)}) copy-start(bf16[768,768]{1,0:T(8,128)(2,1)} %param.25) | copy-start | bytes 3538948
  88.3 102.6 %all-reduce.18.cloned.1.call-start = ((), (), s32[]{:S(2)}) async-start(), calls=%async_computation.6 | async-start | bytes 3145728 | tf_op jit(solution)/shard_map/psum | solution.py:147
  136.5 4.3 copy-start.67
  140.1 4.0 copy-start.7
  140.1 4.0 copy-start.49
  147.8 145.4 %all-reduce.20.cloned.1.call-start = ((), (), s32[]{:S(2)}) async-start(), calls=%async_computation.7 | async-start | bytes 3145728 | tf_op jit(solution)/shard_map/psum | solution.py:181
  148.6 46.8 %copy-start.39 = (f32[1024]{0:T(1024)S(1)}, f32[1024]{0:T(1024)}, u32[]{:S(2)}) copy-start(f32[1024]{0:T(1024)} %copy-done.38) | copy-start | bytes 12292
  148.6 46.8 %copy-start.21 = (f32[768]{0:T(1024)S(1)}, f32[768]{0:T(1024)}, u32[]{:S(2)}) copy-start(f32[768]{0:T(1024)} %copy-done.20) | copy-start | bytes 9220
  148.6 46.8 %copy-start.24 = (f32[1024]{0:T(1024)S(1)}, f32[1024]{0:T(1024)}, u32[]{:S(2)}) copy-start(f32[1024]{0:T(1024)} %copy-done.23) | copy-start | bytes 12292
  148.6 46.8 %copy-start.28 = (f32[768]{0:T(1024)S(1)}, f32[768]{0:T(1024)}, u32[]{:S(2)}) copy-start(f32[768]{0:T(1024)} %copy-done.27) | copy-start | bytes 9220
  148.7 46.8 %copy-start.31 = (f32[1024]{0:T(1024)S(1)}, f32[1024]{0:T(1024)}, u32[]{:S(2)}) copy-start(f32[1024]{0:T(1024)} %copy-done.30) | copy-start | bytes 12292
  190.9 4.5 copy-start.5
  202.9 5.4 copy-start.14
  202.9 5.4 copy-start.41
  202.9 9.9 %slice-start = ((s8[6291456]{0:T(1024)(128)(4,1)}), s8[4194304]{0:T(1024)(128)(4,1)S(1)}, s32[]{:S(2)}) async-start(s8[6291456]{0:T(1024)(128)(4,1)} %bitcast.84), calls=%async_computation.12 | async-start | bytes 8388608
  208.3 4.6 slice-start.1
  223.6 108.8 %reduce-scatter.17.cloned.1.call-start = ((), (), s32[]{:S(2)}) async-start(), calls=%async_computation.11 | async-start | bytes 884736
  230.3 171.6 %reduce-scatter.15.cloned.1.call-start = ((), (), s32[]{:S(2)}) async-start(), calls=%async_computation.10 | async-start | bytes 2211840
  235.8 5.6 %copy-start.22 = (f32[768]{0:T(1024)S(1)}, f32[768]{0:T(1024)}, u32[]{:S(2)}) copy-start(f32[768]{0:T(1024)} %copy-done.20) | copy-start | bytes 9220
  235.8 5.6 %copy-start.25 = (f32[1024]{0:T(1024)S(1)}, f32[1024]{0:T(1024)}, u32[]{:S(2)}) copy-start(f32[1024]{0:T(1024)} %copy-done.23) | copy-start | bytes 12292
  235.8 5.6 %copy-start.29 = (f32[768]{0:T(1024)S(1)}, f32[768]{0:T(1024)}, u32[]{:S(2)}) copy-start(f32[768]{0:T(1024)} %copy-done.27) | copy-start | bytes 9220
  235.8 5.6 %copy-start.32 = (f32[1024]{0:T(1024)S(1)}, f32[1024]{0:T(1024)}, u32[]{:S(2)}) copy-start(f32[1024]{0:T(1024)} %copy-done.30) | copy-start | bytes 12292
  235.8 5.6 %copy-start.48 = (f32[768]{0:T(1024)S(1)}, f32[768]{0:T(1024)}, u32[]{:S(2)}) copy-start(f32[768]{0:T(1024)} %convert_element_type.130) | copy-start | bytes 9220
  235.8 238.3 %reduce-scatter.13.cloned.1.call-start = ((), (), s32[]{:S(2)}) async-start(), calls=%async_computation.9 | async-start | bytes 2654208 | tf_op jit(solution)/shard_map/reduce_scatter | solution.py:207
  241.3 5.5 copy-start.64
  241.3 7.3 %copy-start.61 = (bf16[768]{0:T(1024)(128)(2,1)S(1)}, bf16[768]{0:T(1024)(128)(2,1)}, u32[]{:S(2)}) copy-start(bf16[768]{0:T(1024)(128)(2,1)} %param.28) | copy-start | bytes 4612
  241.3 7.3 %copy-start.55 = (f32[768]{0:T(1024)S(1)}, f32[768]{0:T(1024)}, u32[]{:S(2)}) copy-start(f32[768]{0:T(1024)} %get-tuple-element.86) | copy-start | bytes 9220
  241.3 7.4 %copy-start.35 = (f32[768]{0:T(1024)S(1)}, f32[768]{0:T(1024)}, u32[]{:S(2)}) copy-start(f32[768]{0:T(1024)} %convert_element_type.136) | copy-start | bytes 9220
  241.3 305.1 %reduce-scatter.11.cloned.1.call-start = ((), (), s32[]{:S(2)}) async-start(), calls=%async_computation.8 | async-start | bytes 2654208 | tf_op jit(solution)/shard_map/reduce_scatter | solution.py:205
  246.7 4.0 copy-start.53
  246.7 4.0 copy-start.42
  246.7 4.0 copy-start.44
  246.7 4.1 copy-start.45
  246.7 4.1 copy-start.46
  246.7 4.1 copy-start.51
  246.7 4.1 copy-start.52
  246.7 299.7 %copy-start.1 = (bf16[768,768]{1,0:T(8,128)(2,1)S(1)}, bf16[768,768]{1,0:T(8,128)(2,1)}, u32[]{:S(2)}) copy-start(bf16[768,768]{1,0:T(8,128)(2,1)} %param.23) | copy-start | bytes 3538948
  (31 other events, 77.1 us)
Sparse Core Ops, SparseCore 0:
  25.3 45.5 all-reduce.13
  88.4 42.8 all-reduce.15
  147.9 42.8 all-reduce.17
  223.7 42.9 all-reduce.19
  269.8 62.5 reduce-scatter.16
  336.2 65.7 reduce-scatter.14
  406.0 68.0 reduce-scatter.12
  478.2 68.1 reduce-scatter.10
where the time goes:
time: 560 us; the launch traced here: 553 us
  waiting for transfers between devices  374 us (67%)
  matrix products  58.2 us (10%)
  blocking collectives  37.6 us (7%)
  other arithmetic  33.5 us (6%)
  local copies, waits for them, and re-layouts  33.2 us (6%)
  between operations  16.7 us (3%)
    unnamed x10, waiting for transfers between devices  105 us
    reduce_scatter x1, waiting for transfers between devices, body(): lax.psum_scatter(up_grad, 'dp', scatter_dimension=0, tiled=True)  72.3 us
    reduce_scatter x1, waiting for transfers between devices, body(): lax.psum_scatter(down_grad, 'dp', scatter_dimension=1, tiled=True)  70.4 us
    psum x1, waiting for transfers between devices, body(): lax.psum(attn_terms.astype(jnp.bfloat16), 'tensor').astype(jnp.float32)  43.2 us
    psum x1, waiting for transfers between devices, body(): lax.psum(up_terms.astype(jnp.bfloat16), 'tensor').astype(jnp.float32)  42.2 us
    psum x1, waiting for transfers between devices, body(): lax.psum(down_terms.astype(jnp.bfloat16), 'tensor').astype(jnp.float32)  40.5 us
    unnamed x1, blocking collectives  37.6 us
    unnamed x161, local copies, waits for them, and re-layouts  25.7 us
  transfers between devices with their start and end apart: 8, of which 7 were waited for; matrix products, arithmetic and copies ran while one was open for 7% of the time, Pallas kernels for 0%

commit v1 on v0

--- a/solution.py
+++ b/solution.py
@@ -1,11 +1,20 @@
+import functools
 import jax
 import jax.numpy as jnp
 from jax import lax
 from jax.sharding import PartitionSpec as P
+from jax.lax import all_gather
 
 HEAD = 64
 SEQ = 512
 EPS = 1e-12
+
+
+def form_squares_over_axis(frame_in, across):
+    return jnp.sum(all_gather(frame_in, axis_name=across), axis=0)
+
+
+lead_wires = functools.partial(form_squares_over_axis, across="tensor")
 
 
 def normalize(rows_in, gain_vec, shift_vec):
@@ -144,7 +153,7 @@
     d_hidden_low = d_hidden.astype(jnp.bfloat16)
     up_grad = jnp.einsum("td,tf->df", first_low, d_hidden_low, preferred_element_type=jnp.float32)
     up_terms = jnp.einsum("tf,df->td", d_hidden_low, up_weight, preferred_element_type=jnp.float32)
-    up_total = lax.psum(up_terms.astype(jnp.bfloat16), "tensor").astype(jnp.float32)
+    up_total = lead_wires(up_terms.astype(jnp.bfloat16)).astype(jnp.float32)
     d_first = d_second + up_total
     d_first_in, gain_first_grad, shift_first_grad = norm_back(
         first_in, gain_first, shift_first, d_first

time: 560 us -> 569 us (1.016)
    all_gather x0 -> x1, waiting for transfers between devices: none -> 45.8 us  [form_squares_over_axis(): return jnp.sum(all_gather(frame_in, axis_name=across), axis=0)]
    psum x1 -> x0, waiting for transfers between devices: 42.2 us -> none  [body(): lax.psum(up_terms.astype(jnp.bfloat16), 'tensor').astype(jnp.float32)]
    unnamed x161 -> x163, local copies, waits for them, and re-layouts: 25.7 us -> 25.6 us
where the time goes in v1:
time: 569 us; the launch traced here: 562 us
  waiting for transfers between devices  377 us (66%)
  matrix products  58.3 us (10%)
  other arithmetic  39 us (7%)
  blocking collectives  37.5 us (7%)
  local copies, waits for them, and re-layouts  33.2 us (6%)
  between operations  16.6 us (3%)
    unnamed x10, waiting for transfers between devices  105 us
    reduce_scatter x1, waiting for transfers between devices, body(): lax.psum_scatter(up_grad, 'dp', scatter_dimension=0, tiled=True)  72.1 us
    reduce_scatter x1, waiting for transfers between devices, body(): lax.psum_scatter(down_grad, 'dp', scatter_dimension=1, tiled=True)  70.4 us
    all_gather x1, waiting for transfers between devices, form_squares_over_axis(): return jnp.sum(all_gather(frame_in, axis_name=across), axis=0)  45.8 us
    psum x1, waiting for transfers between devices, body(): lax.psum(attn_terms.astype(jnp.bfloat16), 'tensor').astype(jnp.float32)  43.2 us
    psum x1, waiting for transfers between devices, body(): lax.psum(down_terms.astype(jnp.bfloat16), 'tensor').astype(jnp.float32)  40.5 us
    unnamed x1, blocking collectives  37.5 us
    unnamed x163, local copies, waits for them, and re-layouts  25.6 us
  transfers between devices with their start and end apart: 8, of which 7 were waited for; matrix products, arithmetic and copies ran while one was open for 7% of the time, Pallas kernels for 0%

profile of v1, /device:TPU:0, one launch (start us, length us, event | category | flops | bytes accessed | tf_op | source)
XLA Modules:
  0.0 562.4 jit_solution(16559771452155627336)
XLA Ops:
  7.2 2.8 fusion.21
  11.2 1.2 broadcast_compare_fusion
  13.4 2.1 squeeze.8
  15.5 2.5 fusion.66
  19.0 1.7 copy-done.2
  20.7 1.3 fusion.29
  23.3 1.8 convolution_convert_fusion.3
  25.7 1.3 convert_element_type.132
  27.6 43.2 %all-reduce.13.cloned.1.call-done = bf16[1024,768]{1,0:T(8,128)(2,1)} async-done(((bf16[1024,768]{1,0:T(8,128)(2,1)}), bf16[1024,768]{1,0:T(8,128)(2,1)}) %all-reduce.13.cloned.1.call-update) | async-done | bytes 1572880 | tf_op jit(solution)/shard_map/psum | solution.py:125
  70.8 2.1 fusion.17
  74.5 9.9 %multiply_convert_fusion.1 = (bf16[1024,768]{1,0:T(8,128)(2,1)S(1)}, f32[1024,768]{1,0:T(8,128)}, f32[1024,768]{1,0:T(8,128)}) fusion(f32[768]{0:T(1024)S(1)} %copy-done.58, bf16[768,768]{1,0:T(8,128)(2,1)S(1)} %copy-done, f32[768]{0:T(1024)S(1)} %copy-done.47, f32[768]{0:T(1024)S(1)} %convert_element_type.131, f32[1024]{0:T(1024)S(1)} %fusion.49, ...), kind=kOutput, calls=%fused_computation.27 | convolution fusion | flops 1266941952 | bytes 12210176 | tf_op jit(solution)/shard_map/dot_general | solution.py:131
  84.4 1.2 copy-done.66
  85.5 2.6 convolution_convert_fusion.2
  88.2 1.3 convert_element_type.138
  89.5 1.3 convert_element_type.137
  90.7 40.5 %all-reduce.15.cloned.1.call-done = bf16[1024,768]{1,0:T(8,128)(2,1)} async-done(((bf16[1024,768]{1,0:T(8,128)(2,1)}), bf16[1024,768]{1,0:T(8,128)(2,1)}) %all-reduce.15.cloned.1.call-update) | async-done | bytes 1572880 | tf_op jit(solution)/shard_map/psum | solution.py:137
  131.2 3.3 fusion.62
  134.5 1.8 fusion.4
  136.4 3.6 fusion.61
  140.7 3.2 fusion.69
  143.9 1.2 copy-done.69
  145.1 2.7 convolution_convert_fusion.1
  148.6 45.8 %all-gather.3.cloned.1.call-done = bf16[4096,768]{1,0:T(8,128)(2,1)} async-done(((bf16[1024,768]{1,0:T(8,128)(2,1)}), bf16[4096,768]{1,0:T(8,128)(2,1)}) %all-gather.3.cloned.1.call-update) | async-done | bytes 6291472 | tf_op jit(solution)/shard_map/all_gather | solution.py:14
  194.4 5.4 reduce_sum.191
  199.8 4.6 fusion.59
  204.4 2.7 multiply_reduce_fusion.1
  207.1 2.1 fusion.60
  209.2 1.7 copy-done.6
  211.9 5.4 fusion.67
  217.3 4.5 multiply_reduce_fusion
  221.9 1.8 multiply_convert_fusion
  223.7 1.1 fusion.26
  228.8 3.9 convolution_convert_fusion
  232.7 2.4 fusion.19
  235.1 1.5 copy.79
  236.6 2.8 reshape.191
  239.5 2.3 convolution_bitcast_fusion
  241.8 3.0 copy.83
  244.9 5.4 fusion.51
  250.5 5.2 fusion.37
  257.8 2.0 fusion.32
  259.8 37.5 %all-reduce.8 = (f32[2,3,64]{2,1,0:T(4,128)S(1)}, f32[768]{0:T(1024)S(1)}, f32[768]{0:T(1024)S(1)}, f32[768]{0:T(1024)S(1)}, f32[12,64]{1,0:T(8,128)S(1)}, /*ind...) all-reduce(f32[2,3,64]{2,1,0:T(4,128)S(1)} %pad_maximum_fusion, ...), channel_id=4, replica_groups=mesh['dp'=8,'tensor'=4] {'dp'}, use_global_device_ids=true, to_apply=%region_18.19.clone | all-reduce | flops 5760 | bytes 46080
  302.2 2.1 fusion.30
  304.2 37.2 %reduce-scatter.17.cloned.1.call-done = f32[96,192]{1,0:T(8,128)} async-done(((f32[768,192]{1,0:T(8,128)}), f32[96,192]{1,0:T(8,128)}) %reduce-scatter.17.cloned.1.call-update) | async-done | bytes 73744
  343.2 67.7 %reduce-scatter.15.cloned.1.call-done = f32[96,576]{1,0:T(8,128)} async-done(((f32[768,576]{1,0:T(8,128)}), f32[96,576]{1,0:T(8,128)}) %reduce-scatter.15.cloned.1.call-update) | async-done | bytes 221200
  410.9 1.8 copy.84
  412.7 70.4 %reduce-scatter.13.cloned.1.call-done = f32[768,96]{0,1:T(8,128)} async-done(((f32[768,768]{0,1:T(8,128)}), f32[768,96]{0,1:T(8,128)}) %reduce-scatter.13.cloned.1.call-update) | async-done | bytes 294928 | tf_op jit(solution)/shard_map/reduce_scatter | solution.py:216
  483.2 72.1 %reduce-scatter.11.cloned.1.call-done = f32[96,768]{1,0:T(8,128)} async-done(((f32[768,768]{1,0:T(8,128)}), f32[96,768]{1,0:T(8,128)}) %reduce-scatter.11.cloned.1.call-update) | async-done | bytes 294928 | tf_op jit(solution)/shard_map/reduce_scatter | solution.py:214
  (205 shorter events, 21.2 us)
Async XLA Ops:
  7.2 67.3 %copy-start = (bf16[768,768]{1,0:T(8,128)(2,1)S(1)}, bf16[768,768]{1,0:T(8,128)(2,1)}, u32[]{:S(2)}) copy-start(bf16[768,768]{1,0:T(8,128)(2,1)} %param.23) | copy-start | bytes 3538948
  7.2 63.6 %all-reduce.13.cloned.1.call-start = ((), (), s32[]{:S(2)}) async-start(), calls=%async_computation.4 | async-start | bytes 3145728 | tf_op jit(solution)/shard_map/psum | solution.py:125
  12.7 5.3 copy-start.9
  13.4 5.6 copy-start.13
  22.0 4.9 copy-start.57
  22.0 48.8 %copy-start.3 = (bf16[1024,768]{1,0:T(8,128)(2,1)S(1)}, bf16[1024,768]{1,0:T(8,128)(2,1)}, u32[]{:S(2)}) copy-start(bf16[1024,768]{1,0:T(8,128)(2,1)} %param.15) | copy-start | bytes 4718596
  25.1 106.1 %all-reduce.15.cloned.1.call-start = ((), (), s32[]{:S(2)}) async-start(), calls=%async_computation.5 | async-start | bytes 3145728 | tf_op jit(solution)/shard_map/psum | solution.py:137
  25.7 105.5 %copy-start.20 = (f32[768]{0:T(1024)}, f32[768]{0:T(1024)S(1)}, u32[]{:S(2)}) copy-start(f32[768]{0:T(1024)S(1)} %convert_element_type.130) | copy-start | bytes 9220
  25.7 105.5 %copy-start.27 = (f32[768]{0:T(1024)}, f32[768]{0:T(1024)S(1)}, u32[]{:S(2)}) copy-start(f32[768]{0:T(1024)S(1)} %convert_element_type.131) | copy-start | bytes 9220
  72.9 58.2 %copy-start.23 = (f32[1024]{0:T(1024)}, f32[1024]{0:T(1024)S(1)}, u32[]{:S(2)}) copy-start(f32[1024]{0:T(1024)S(1)} %broadcast_multiply_fusion.1) | copy-start | bytes 12292
  74.5 56.7 %copy-start.30 = (f32[1024]{0:T(1024)}, f32[1024]{0:T(1024)S(1)}, u32[]{:S(2)}) copy-start(f32[1024]{0:T(1024)S(1)} %fusion.49) | copy-start | bytes 12292
  74.5 11.1 %copy-start.63 = (bf16[768,768]{1,0:T(8,128)(2,1)S(1)}, bf16[768,768]{1,0:T(8,128)(2,1)}, u32[]{:S(2)}) copy-start(bf16[768,768]{1,0:T(8,128)(2,1)} %param.25) | copy-start | bytes 3538948
  88.1 106.3 %all-gather.3.cloned.1.call-start = ((), (), s32[]{:S(2)}) async-start(), calls=%async_computation.9 | async-start | bytes 7864320 | tf_op jit(solution)/shard_map/all_gather | solution.py:14
  136.3 4.3 copy-start.68
  139.9 4.0 copy-start.7
  147.8 154.4 %all-reduce.17.cloned.1.call-start = ((), (), s32[]{:S(2)}) async-start(), calls=%async_computation.6 | async-start | bytes 3145728 | tf_op jit(solution)/shard_map/psum | solution.py:190
  194.4 5.4 copy-start.21
  194.4 5.4 copy-start.24
  194.4 5.4 copy-start.28
  194.4 5.4 copy-start.50
  199.8 4.6 copy-start.39
  199.8 4.6 copy-start.5
  199.8 4.6 copy-start.31
  211.9 5.4 copy-start.14
  211.9 5.4 copy-start.41
  211.9 9.9 %slice-start = ((s8[6291456]{0:T(1024)(128)(4,1)}), s8[4194304]{0:T(1024)(128)(4,1)S(1)}, s32[]{:S(2)}) async-start(s8[6291456]{0:T(1024)(128)(4,1)} %bitcast.85), calls=%async_computation.12 | async-start | bytes 8388608
  217.3 4.6 slice-start.1
  232.6 108.8 %reduce-scatter.17.cloned.1.call-start = ((), (), s32[]{:S(2)}) async-start(), calls=%async_computation.11 | async-start | bytes 884736
  239.4 171.5 %reduce-scatter.15.cloned.1.call-start = ((), (), s32[]{:S(2)}) async-start(), calls=%async_computation.10 | async-start | bytes 2211840
  244.8 5.6 copy-start.22
  244.8 5.6 copy-start.25
  244.8 5.6 copy-start.29
  244.9 5.6 copy-start.32
  244.9 5.6 copy-start.48
  244.9 238.3 %reduce-scatter.13.cloned.1.call-start = ((), (), s32[]{:S(2)}) async-start(), calls=%async_computation.8 | async-start | bytes 2654208 | tf_op jit(solution)/shard_map/reduce_scatter | solution.py:216
  250.3 5.5 copy-start.65
  250.3 7.4 %copy-start.62 = (bf16[768]{0:T(1024)(128)(2,1)S(1)}, bf16[768]{0:T(1024)(128)(2,1)}, u32[]{:S(2)}) copy-start(bf16[768]{0:T(1024)(128)(2,1)} %param.28) | copy-start | bytes 4612
  250.4 7.4 %copy-start.56 = (f32[768]{0:T(1024)S(1)}, f32[768]{0:T(1024)}, u32[]{:S(2)}) copy-start(f32[768]{0:T(1024)} %get-tuple-element.86) | copy-start | bytes 9220
  250.4 7.4 %copy-start.35 = (f32[768]{0:T(1024)S(1)}, f32[768]{0:T(1024)}, u32[]{:S(2)}) copy-start(f32[768]{0:T(1024)} %convert_element_type.138) | copy-start | bytes 9220
  250.4 304.9 %reduce-scatter.11.cloned.1.call-start = ((), (), s32[]{:S(2)}) async-start(), calls=%async_computation.7 | async-start | bytes 2654208 | tf_op jit(solution)/shard_map/reduce_scatter | solution.py:214
  255.7 4.0 copy-start.54
  255.7 4.0 copy-start.42
  255.7 4.1 copy-start.44
  255.7 4.1 copy-start.45
  255.7 4.1 copy-start.46
  255.7 4.1 copy-start.52
  255.7 4.1 copy-start.53
  255.8 299.5 %copy-start.1 = (bf16[768,768]{1,0:T(8,128)(2,1)S(1)}, bf16[768,768]{1,0:T(8,128)(2,1)}, u32[]{:S(2)}) copy-start(bf16[768,768]{1,0:T(8,128)(2,1)} %param.23) | copy-start | bytes 3538948
  (32 other events, 81.1 us)
Sparse Core Ops, SparseCore 0:
  25.2 45.5 all-reduce.12
  88.2 42.8 all-reduce.14
  147.9 46.4 all-gather.2
  232.8 42.8 all-reduce.16
  278.8 62.5 reduce-scatter.16
  345.2 65.6 reduce-scatter.14
  415.0 68.1 reduce-scatter.12
  487.2 68.0 reduce-scatter.10
